TPU v7x, 32 devices: a whole 2x2x4 slice. The times are simulated.
32 devices in a mesh: sample: 2 (over core), outer: 2 (over y), inner: 8 (over z, x).
Axes of the slice: x: 2, y: 2, z: 4, core: 2. Of those that a mesh axis runs over, the one named last changes fastest.
Arguments:
- out_cotangent: bfloat16 [32, 384, 1152], P(('sample', 'outer', 'inner')), parts along dimension 0, may hold values from -6 to 6
- wo_spatial: bfloat16 [576, 1152], replicated, may hold values from -0.75 to 0.75
- wqkv_spatial: bfloat16 [1152, 1728], replicated, may hold values from -0.1875 to 0.1875
- wo_temporal: bfloat16 [576, 1152], replicated, may hold values from -0.75 to 0.75
- q_spatial: bfloat16 [32, 384, 576], P(('sample', 'outer', 'inner')), parts along dimension 0, may hold values from -6 to 6
- k_spatial: bfloat16 [32, 384, 576], P(('sample', 'outer', 'inner')), parts along dimension 0, may hold values from -6 to 6
- v_spatial: bfloat16 [32, 384, 576], P(('sample', 'outer', 'inner')), parts along dimension 0, may hold values from -6 to 6
- q_temporal: bfloat16 [32, 384, 576], P('sample', ('outer', 'inner')), parts along dimension 0, may hold values from -6 to 6
- k_temporal: bfloat16 [32, 384, 576], P('sample', ('outer', 'inner')), parts along dimension 0, may hold values from -6 to 6
- v_temporal: bfloat16 [32, 384, 576], P('sample', ('outer', 'inner')), parts along dimension 0, may hold values from -6 to 6
Outputs:
- middle_grad: bfloat16 [32, 384, 1152], P(('sample', 'outer', 'inner')), parts along dimension 0
- temporal_grads: bfloat16 [32, 384, 1728], P(('sample', 'outer', 'inner')), parts along dimension 0
There are 2 independent parts, one for each index of `sample`. A program takes and returns all parts, laid end to end along the dimension named above; an argument that names none is the same for every part. Nothing has to cross between parts.
All inputs are finite; a program needn't handle non-finite values.
Results may differ from a plain program's by a relative error of at most 0.015.
Values may be sent and summed in bfloat16 or wider, within the bound.
No kernel may reach another device: no remote copies, remote signals or barrier semaphores. Data moves between devices by JAX's collectives and lax.ppermute only.
A program may use at most 64 MiB of HBM per device.

v0:
```python
import jax
import jax.numpy as jnp
from jax import lax
from jax.sharding import PartitionSpec as P

HEADS = 8


def attend_back(queries, key_rows, value_rows, grad_out):
    scaling = queries.shape[-1] ** (-0.5)
    scores = (
        jnp.einsum("lbhe,mbhe->bhlm", queries, key_rows, preferred_element_type=jnp.float32)
        * scaling
    )
    row_max = jnp.max(scores, axis=-1, keepdims=True)
    weights = jnp.exp(scores - row_max)
    weights = weights / jnp.sum(weights, axis=-1, keepdims=True)
    weights_low = weights.astype(jnp.bfloat16)
    grad_value = jnp.einsum(
        "bhlm,lbhe->mbhe", weights_low, grad_out, preferred_element_type=jnp.float32
    ).astype(jnp.bfloat16)
    grad_weight = jnp.einsum(
        "lbhe,mbhe->bhlm", grad_out, value_rows, preferred_element_type=jnp.float32
    )
    row_inner = jnp.sum(weights * grad_weight, axis=-1, keepdims=True)
    grad_score = (weights * (grad_weight - row_inner)).astype(jnp.bfloat16)
    grad_query = (
        jnp.einsum("bhlm,mbhe->lbhe", grad_score, key_rows, preferred_element_type=jnp.float32)
        * scaling
    ).astype(jnp.bfloat16)
    grad_key = (
        jnp.einsum("bhlm,lbhe->mbhe", grad_score, queries, preferred_element_type=jnp.float32)
        * scaling
    ).astype(jnp.bfloat16)
    return (grad_query, grad_key, grad_value)


def heads_view(array, length, batch):
    return array.reshape(length, batch, HEADS, array.shape[-1] // HEADS)


def local(
    out_cotangent,
    wo_spatial,
    wqkv_spatial,
    wo_temporal,
    q_spatial,
    k_spatial,
    v_spatial,
    q_temporal,
    k_temporal,
    v_temporal,
):
    tokens = out_cotangent.shape[1]
    features = out_cotangent.shape[2]
    channels = q_spatial.shape[2]
    contract = (((1,), (1,)), ((), ()))
    grad_rows = out_cotangent.reshape(tokens, features)
    spatial_out = lax.dot_general(
        grad_rows, wo_spatial, contract, preferred_element_type=jnp.float32
    ).astype(jnp.bfloat16)
    spatial_query, spatial_key, spatial_value = attend_back(
        heads_view(q_spatial, tokens, 1),
        heads_view(k_spatial, tokens, 1),
        heads_view(v_spatial, tokens, 1),
        heads_view(spatial_out, tokens, 1),
    )
    spatial_grads = jnp.concatenate(
        [
            spatial_query.reshape(tokens, channels),
            spatial_key.reshape(tokens, channels),
            spatial_value.reshape(tokens, channels),
        ],
        axis=1,
    )
    spatial_term = lax.dot_general(
        spatial_grads, wqkv_spatial, contract, preferred_element_type=jnp.float32
    )
    middle = (grad_rows.astype(jnp.float32) + spatial_term).astype(jnp.bfloat16)
    groups = lax.axis_size(("outer", "inner"))
    pos_dev = tokens // groups
    projected = lax.dot_general(
        middle, wo_temporal, contract, preferred_element_type=jnp.float32
    ).astype(jnp.bfloat16)
    temporal_out = lax.all_to_all(
        projected.reshape(groups, pos_dev, channels),
        ("outer", "inner"),
        split_axis=0,
        concat_axis=0,
        tiled=True,
    )
    frames = q_temporal.shape[0]
    temporal_query, temporal_key, temporal_value = attend_back(
        heads_view(q_temporal, frames, pos_dev),
        heads_view(k_temporal, frames, pos_dev),
        heads_view(v_temporal, frames, pos_dev),
        heads_view(temporal_out, frames, pos_dev),
    )
    stacked = jnp.concatenate(
        [
            temporal_query.reshape(frames, pos_dev, channels),
            temporal_key.reshape(frames, pos_dev, channels),
            temporal_value.reshape(frames, pos_dev, channels),
        ],
        axis=2,
    )
    returned = lax.all_to_all(stacked, ("outer", "inner"), split_axis=0, concat_axis=0, tiled=True)
    return (middle.reshape(1, tokens, features), returned.reshape(1, tokens, 3 * channels))


def solution(mesh):
    return jax.shard_map(
        local,
        mesh=mesh,
        in_specs=(
            P(("sample", "outer", "inner"), None, None),
            P(),
            P(),
            P(),
            P(("sample", "outer", "inner"), None, None),
            P(("sample", "outer", "inner"), None, None),
            P(("sample", "outer", "inner"), None, None),
            P("sample", ("outer", "inner"), None),
            P("sample", ("outer", "inner"), None),
            P("sample", ("outer", "inner"), None),
        ),
        out_specs=(
            P(("sample", "outer", "inner"), None, None),
            P(("sample", "outer", "inner"), None, None),
        ),
        check_vma=False,
    )
```

profile of v0, /device:TPU:0, one launch (start us, length us, event | category | flops | bytes accessed | tf_op | source)
XLA Modules:
  0.0 96.9 jit_solution(14263435843078967887)
XLA Ops:
  0.7 5.0 %fusion.48 = (f32[8,384]{1,0:T(8,128)S(1)}, f32[8,384,384]{1,2,0:T(8,128)}) fusion(bf16[384,8,72]{0,2,1:T(8,128)(2,1)} %bitcast.62, bf16[384,8,72]{0,2,1:T(8,128)(2,1)} %bitcast.64), kind=kOutput, calls=%fused_computation.52 | convolution fusion | flops 173408640 | bytes 5615616 | tf_op jit(solution)/shard_map/sub | solution.py:16
  5.6 0.9 convolution_convert_fusion.2
  6.6 3.3 %multiply_reduce_fusion = (f32[8,384]{1,0:T(8,128)S(1)}, f32[8,384,384]{1,2,0:T(8,128)S(1)}) fusion(f32[8,384,384]{1,2,0:T(8,128)} %get-tuple-element.5, f32[8,384]{1,0:T(8,128)S(1)} %get-tuple-element.4, bf16[384,8,72]{0,2,1:T(8,128)(2,1)S(1)} %bitcast.70, bf16[384,8,72]{0,2,1:T(8,128)(2,1)S(1)} %bitcast.68), kind=kOutput, calls=%fused_computation.3 | convolution fusion | flops 173405184 | bytes 10346496 | tf_op jit(solution)/shard_map/lbhe,mbhe->bhlm/dot_general | solution.py:22
  10.3 0.7 multiply_convert_fusion
  11.0 0.3 copy-done.5
  11.3 1.1 %fusion.23 = bf16[8,384,72]{1,2,0:T(8,128)(2,1)S(1)} fusion(bf16[8,384,384]{1,2,0:T(8,128)(2,1)S(1)} %multiply_convert_fusion, bf16[384,8,72]{0,2,1:T(8,128)(2,1)S(1)} %bitcast.63), kind=kOutput, calls=%fused_computation.33 | convolution fusion | flops 170311680 | bytes 3244032 | tf_op jit(solution)/shard_map/bhlm,lbhe->mbhe/dot_general | solution.py:32
  12.4 0.5 fusion.22
  12.9 1.1 %fusion.19 = bf16[8,72,384]{2,1,0:T(8,128)(2,1)S(1)} fusion(bf16[384,8,72]{0,2,1:T(8,128)(2,1)S(1)} %bitcast.71, f32[8,384,384]{1,2,0:T(8,128)S(1)} %bitcast.61, f32[8,384]{1,0:T(8,128)S(1)} %get-tuple-element.4), kind=kOutput, calls=%fused_computation.31 | convolution fusion | flops 172449792 | bytes 5615616 | tf_op jit(solution)/shard_map/bhlm,lbhe->mbhe/dot_general | solution.py:19
  14.0 1.0 %copy-done.7 = bf16[1152,1728]{0,1:T(8,128)(2,1)S(1)} copy-done((bf16[1152,1728]{0,1:T(8,128)(2,1)S(1)}, bf16[1152,1728]{0,1:T(8,128)(2,1)}, u32[]{:S(2)}) %copy-start.7) | copy-done | bytes 3981336
  15.0 2.0 %fusion.5 = bf16[384,1152]{1,0:T(8,128)(2,1)S(1)} fusion(bf16[1152,1728]{0,1:T(8,128)(2,1)S(1)} %copy-done.7, bf16[384,576]{0,1:T(8,128)(2,1)S(1)} %bitcast.72, bf16[384,576]{0,1:T(8,128)(2,1)S(1)} %bitcast.66, bf16[384,576]{0,1:T(8,128)(2,1)S(1)} %bitcast.67, bf16[1,384,1152]{2,1,0:T(8,128)(2,1)S(1)} %copy-done.9), kind=kOutput, calls=%fused_computation.8 | convolution fusion | flops 1534132224 | bytes 7077888 | tf_op jit(solution)/shard_map/dot_general | solution.py:76
  17.1 0.9 copy-done.11
  18.0 0.9 convolution_convert_fusion.1
  18.9 1.0 %copy.26 = bf16[384,576]{1,0:T(8,128)(2,1)} copy(bf16[384,576]{0,1:T(8,128)(2,1)S(1)} %convolution_convert_fusion.1) | data formatting | bytes 884736 | tf_op jit(solution)/shard_map/convert_element_type | solution.py:84
  19.9 8.3 %all-to-all-start = ((bf16[16,24,576]{2,1,0:T(8,128)(2,1)}), bf16[16,24,576]{2,1,0:T(8,128)(2,1)S(1)}, u32[]{:S(2)}, u32[]{:S(2)}) async-start(bf16[16,24,576]{2,1,0:T(8,128)(2,1)} %bitcast.17), calls=%async_computation | async-start | bytes 983040 | tf_op jit(solution)/shard_map/all_to_all | solution.py:85
  28.2 0.8 reshape.126
  29.0 1.9 %reshape.127 = bf16[16,24,8,72]{3,2,1,0:T(8,128)(2,1)S(1)} reshape(bf16[16,24,576]{2,1,0:T(8,128)(2,1)} %param.18) | data formatting | bytes 884736 | tf_op jit(solution)/shard_map/reshape | solution.py:39
  31.0 2.6 %reshape.130 = bf16[16,24,8,72]{3,2,1,0:T(8,128)(2,1)} reshape(bf16[16,24,576]{2,1,0:T(8,128)(2,1)} %param.19) | data formatting | bytes 884736 | tf_op jit(solution)/shard_map/reshape | solution.py:39
  33.6 2.6 %fusion.49 = (f32[24,8,16]{2,1,0:T(8,128)S(1)}, f32[24,8,16,16]{2,3,1,0:T(8,128)}) fusion(bf16[16,24,8,72]{3,2,1,0:T(8,128)(2,1)S(1)} %reshape.127, bf16[16,24,8,72]{3,2,1,0:T(8,128)(2,1)S(1)} %reshape.126), kind=kOutput, calls=%fused_computation.53 | convolution fusion | flops 7225359 | bytes 1093632 | tf_op jit(solution)/shard_map/sub | solution.py:16
  36.2 6.5 %all-to-all-done = bf16[16,24,576]{2,1,0:T(8,128)(2,1)S(1)} async-done(((bf16[16,24,576]{2,1,0:T(8,128)(2,1)}), bf16[16,24,576]{2,1,0:T(8,128)(2,1)S(1)}, u32[]{:S(2)}, u32[]{:S(2)}) %all-to-all-start) | async-done | bytes 442400 | tf_op jit(solution)/shard_map/all_to_all | solution.py:85
  42.7 1.7 %reshape.129 = bf16[16,24,8,72]{3,2,1,0:T(8,128)(2,1)} reshape(bf16[16,24,576]{2,1,0:T(8,128)(2,1)S(1)} %all-to-all-done) | data formatting | bytes 884736 | tf_op jit(solution)/shard_map/reshape | solution.py:39
  44.4 3.2 %multiply_reduce_fusion.2 = (f32[24,8,16]{2,1,0:T(8,128)S(1)}, f32[24,8,16,16]{2,3,1,0:T(8,128)S(1)}) fusion(f32[24,8,16,16]{2,3,1,0:T(8,128)} %get-tuple-element.9, f32[24,8,16]{2,1,0:T(8,128)S(1)} %get-tuple-element.8, bf16[16,24,8,72]{3,2,1,0:T(8,128)(2,1)} %reshape.130, bf16[16,24,8,72]{3,2,1,0:T(8,128)(2,1)} %reshape.129), kind=kOutput, calls=%fused_computation.17 | convolution fusion | flops 7222272 | bytes 1302528 | tf_op jit(solution)/shard_map/lbhe,mbhe->bhlm/dot_general | solution.py:22
  47.6 0.5 multiply_convert_fusion.3
  48.1 0.7 fusion.18
  48.9 0.7 fusion.17
  49.6 0.4 copy-done.2
  50.0 1.5 %fusion.16 = bf16[16,24,8,72]{3,0,2,1:T(8,128)(2,1)} fusion(bf16[16,24,8,72]{3,2,1,0:T(8,128)(2,1)S(1)} %copy-done.2, f32[24,8,16,16]{2,3,1,0:T(8,128)S(1)} %copy-done.1, f32[24,8,16]{2,1,0:T(8,128)S(1)} %get-tuple-element.8), kind=kOutput, calls=%fused_computation.28 | convolution fusion | flops 7397376 | bytes 1093632 | tf_op jit(solution)/shard_map/bhlm,lbhe->mbhe/dot_general | solution.py:19
  51.7 0.6 reshape.132
  52.5 1.4 %reshape.131 = bf16[16,24,576]{2,1,0:T(8,128)(2,1)} reshape(bf16[16,24,8,72]{3,2,1,0:T(8,128)(2,1)S(1)} %copy.31) | data formatting | bytes 884736 | tf_op jit(solution)/shard_map/reshape | solution.py:101
  54.1 1.4 %reshape.133 = bf16[16,24,576]{2,1,0:T(8,128)(2,1)} reshape(bf16[16,24,8,72]{3,2,1,0:T(8,128)(2,1)S(1)} %copy.35) | data formatting | bytes 884736 | tf_op jit(solution)/shard_map/reshape | solution.py:103
  55.5 2.3 %concatenate.7 = bf16[16,24,1728]{2,1,0:T(8,128)(2,1)S(1)} concatenate(bf16[16,24,576]{2,1,0:T(8,128)(2,1)} %reshape.131, bf16[16,24,576]{2,1,0:T(8,128)(2,1)S(1)} %reshape.132, bf16[16,24,576]{2,1,0:T(8,128)(2,1)} %reshape.133), dimensions={2} | concatenate | bytes 2654208 | tf_op jit(solution)/shard_map/concatenate | solution.py:99
  57.9 36.6 %all_to_all.10 = bf16[16,24,1728]{2,1,0:T(8,128)(2,1)} all-to-all(bf16[16,24,1728]{2,1,0:T(8,128)(2,1)S(1)} %concatenate.7), channel_id=1, replica_groups=mesh['sample'=2,'outer'=2,'inner'=8] {'outer','inner'}, dimensions={0} | all-to-all | bytes 2654208 | tf_op jit(solution)/shard_map/all_to_all | solution.py:107
  94.4 2.5 %copy.36 = bf16[1,384,1728]{1,2,0:T(8,128)(2,1)} copy(bf16[1,384,1728]{2,1,0:T(8,128)(2,1)} %bitcast.59) | data formatting | bytes 2654208
  (28 shorter events, 1.0 us)
Async XLA Ops:
  0.6 5.0 %copy-start = (bf16[576,1152]{1,0:T(8,128)(2,1)S(1)}, bf16[576,1152]{1,0:T(8,128)(2,1)}, u32[]{:S(2)}) copy-start(bf16[576,1152]{1,0:T(8,128)(2,1)} %param.11) | copy-start | bytes 3981316
  0.6 5.0 %copy-start.9 = (bf16[1,384,1152]{2,1,0:T(8,128)(2,1)S(1)}, bf16[1,384,1152]{2,1,0:T(8,128)(2,1)}, u32[]{:S(2)}) copy-start(bf16[1,384,1152]{2,1,0:T(8,128)(2,1)} %param.10) | copy-start | bytes 2654212
  5.6 1.0 %copy-start.10 = (bf16[1,384,576]{1,2,0:T(8,128)(2,1)S(1)}, bf16[1,384,576]{1,2,0:T(8,128)(2,1)}, u32[]{:S(2)}) copy-start(bf16[1,384,576]{1,2,0:T(8,128)(2,1)} %param.16) | copy-start | bytes 1327108
  6.5 3.6 %slice-start = ((s8[4718592]{0:T(1024)(128)(4,1)}), s8[4194304]{0:T(1024)(128)(4,1)S(1)}, s32[]{:S(2)}) async-start(s8[4718592]{0:T(1024)(128)(4,1)} %bitcast.60), calls=%async_computation.2 | async-start | bytes 8388608
  6.6 3.6 %slice-start.1 = ((s8[4718592]{0:T(1024)(128)(4,1)}), s8[524288]{0:T(1024)(128)(4,1)S(1)}, s32[]{:S(2)}) async-start(s8[4718592]{0:T(1024)(128)(4,1)} %bitcast.60), calls=%async_computation.3 | async-start | bytes 1048576
  10.3 1.0 %copy-start.5 = (bf16[1,384,576]{1,2,0:T(8,128)(2,1)S(1)}, bf16[1,384,576]{1,2,0:T(8,128)(2,1)}, u32[]{:S(2)}) copy-start(bf16[1,384,576]{1,2,0:T(8,128)(2,1)} %param.14) | copy-start | bytes 1327108
  11.3 1.1 %copy-start.6 = (bf16[1,384,576]{1,2,0:T(8,128)(2,1)S(1)}, bf16[1,384,576]{1,2,0:T(8,128)(2,1)}, u32[]{:S(2)}) copy-start(bf16[1,384,576]{1,2,0:T(8,128)(2,1)} %param.15) | copy-start | bytes 1327108
  12.9 2.1 %copy-start.7 = (bf16[1152,1728]{0,1:T(8,128)(2,1)S(1)}, bf16[1152,1728]{0,1:T(8,128)(2,1)}, u32[]{:S(2)}) copy-start(bf16[1152,1728]{0,1:T(8,128)(2,1)} %param.12) | copy-start | bytes 11943940
  15.0 3.0 %copy-start.8 = (bf16[576,1152]{1,0:T(8,128)(2,1)S(1)}, bf16[576,1152]{1,0:T(8,128)(2,1)}, u32[]{:S(2)}) copy-start(bf16[576,1152]{1,0:T(8,128)(2,1)} %param.13) | copy-start | bytes 3981316
  17.1 0.9 copy-start.11
  18.9 9.4 %copy-start.4 = (bf16[16,24,576]{2,1,0:T(8,128)(2,1)S(1)}, bf16[16,24,576]{2,1,0:T(8,128)(2,1)}, u32[]{:S(2)}) copy-start(bf16[16,24,576]{2,1,0:T(8,128)(2,1)} %param.17) | copy-start | bytes 1327108
  19.9 22.8 %all-to-all-start = ((bf16[16,24,576]{2,1,0:T(8,128)(2,1)}), bf16[16,24,576]{2,1,0:T(8,128)(2,1)S(1)}, u32[]{:S(2)}, u32[]{:S(2)}) async-start(bf16[16,24,576]{2,1,0:T(8,128)(2,1)} %bitcast.17), calls=%async_computation | async-start | bytes 983040 | tf_op jit(solution)/shard_map/all_to_all | solution.py:85
  44.4 3.2 %copy-start.1 = (f32[24,8,16,16]{2,3,1,0:T(8,128)S(1)}, f32[24,8,16,16]{2,3,1,0:T(8,128)}, u32[]{:S(2)}) copy-start(f32[24,8,16,16]{2,3,1,0:T(8,128)} %get-tuple-element.9) | copy-start | bytes 589828
  48.8 1.1 %copy-start.2 = (bf16[16,24,8,72]{3,2,1,0:T(8,128)(2,1)S(1)}, bf16[16,24,8,72]{3,2,1,0:T(8,128)(2,1)}, u32[]{:S(2)}) copy-start(bf16[16,24,8,72]{3,2,1,0:T(8,128)(2,1)} %reshape.129) | copy-start | bytes 1327108
  52.5 1.4 %copy-start.3 = (bf16[16,24,8,72]{3,0,2,1:T(8,128)(2,1)S(1)}, bf16[16,24,8,72]{3,0,2,1:T(8,128)(2,1)}, u32[]{:S(2)}) copy-start(bf16[16,24,8,72]{3,0,2,1:T(8,128)(2,1)} %fusion.16) | copy-start | bytes 1327108
where the time goes:
time: 97.4 us; the launch traced here: 96.9 us
  blocking collectives  36.6 us (38%)
  matrix products  23.6 us (24%)
  local copies, waits for them, and re-layouts  19.8 us (20%)
  starting transfers between devices  8.35 us (9%)
  waiting for transfers between devices  6.51 us (7%)
  other arithmetic  1.24 us (1%)
    all_to_all x1, blocking collectives, local(): lax.all_to_all(stacked, ('outer', 'inner'), split_axis=0, concat_axis=0,...  36.6 us
    all_to_all x1, starting transfers between devices, local(): lax.all_to_all(projected.reshape(groups, pos_dev, channels), ('outer', 'i...  8.35 us
    sub x2, matrix products, attend_back(): weights = jnp.exp(scores - row_max)  7.6 us
    reshape x4, local copies, waits for them, and re-layouts, heads_view(): return array.reshape(length, batch, HEADS, array.shape[-1] // HEADS)  7.02 us
    dot_general x2, matrix products, attend_back(): jnp.einsum('lbhe,mbhe->bhlm', grad_out, value_rows, preferred_element_typ...  6.55 us
    all_to_all x1, waiting for transfers between devices, local(): lax.all_to_all(projected.reshape(groups, pos_dev, channels), ('outer', 'i...  6.51 us
    unnamed x29, local copies, waits for them, and re-layouts  5.52 us
    dot_general x2, matrix products, attend_back(): jnp.einsum('bhlm,lbhe->mbhe', weights_low, grad_out, preferred_element_ty...  2.64 us
  transfers between devices with their start and end apart: 1, of which 1 were waited for; matrix products, arithmetic and copies ran while one was open for 8% of the time, Pallas kernels for 0%

commit v1 on v0

v1 whole, which is shorter than its diff:
```python
import functools
import math

import jax
import jax.numpy as jnp
from jax import lax
from jax.experimental import pallas as pl
from jax.experimental.pallas import tpu as pltpu
from jax.sharding import PartitionSpec as P

HEADS = 8
F32 = jnp.float32
BF16 = jnp.bfloat16
NN = (((1,), (0,)), ((), ()))
NT = (((1,), (1,)), ((), ()))
TN = (((0,), (0,)), ((), ()))
LOG2E = math.log2(math.e)


def mm(a, b, dims):
    return lax.dot_general(a, b, dims, preferred_element_type=F32)


def spatial_kernel(
    cot_hbm, wos_hbm, wqkv_hbm, wot_hbm, q_hbm, k_hbm, v_hbm,
    mid_hbm, g_hbm,
    cot, wos, wqkv, wot, q, k, v, gs, sg, mid, g, sem,
):
    heads, dim, tokens = q.shape
    channels = heads * dim
    scaling = dim ** (-0.5)
    exp_scale = scaling * LOG2E
    loads = [
        pltpu.make_async_copy(src, dst, sem.at[i])
        for i, (src, dst) in enumerate(
            [(k_hbm, k), (q_hbm, q), (wos_hbm, wos), (cot_hbm, cot), (v_hbm, v),
             (wqkv_hbm, wqkv), (wot_hbm, wot)]
        )
    ]
    for copy in loads:
        copy.start()
    for copy in loads[:5]:
        copy.wait()
    gs[...] = mm(wos[...], cot[...], NT).reshape(heads, dim, tokens)
    for h in range(heads):
        q_t = q[h]
        k_t = k[h]
        keys = k_t.T
        scores = mm(keys, q_t, NN)
        top = jnp.max(scores, axis=0, keepdims=True)
        e = jnp.exp2((scores - top) * exp_scale)
        r = 1.0 / jnp.sum(e, axis=0, keepdims=True)
        e_low = e.astype(BF16)
        g_t = (gs[h] * r).astype(BF16)
        grad_w = mm(v[h].T, g_t, NN)
        inner = jnp.sum(e * grad_w, axis=0, keepdims=True) * r
        ds = (e * (grad_w - inner)).astype(BF16)
        dv = mm(g_t, e_low, NT)
        dk = mm(q_t, ds, NT) * scaling
        dq = mm(k_t, ds, NN) * scaling
        sg[h] = dq.astype(BF16)
        sg[heads + h] = dk.astype(BF16)
        sg[2 * heads + h] = dv.astype(BF16)
    loads[5].wait()
    grads = sg[...].reshape(3 * channels, tokens)
    middle = (cot[...].astype(F32) + mm(grads, wqkv[...], TN)).astype(BF16)
    mid[...] = middle
    out_mid = pltpu.make_async_copy(mid, mid_hbm, sem.at[7])
    out_mid.start()
    loads[6].wait()
    g[...] = mm(middle, wot[...], NT).astype(BF16)
    out_g = pltpu.make_async_copy(g, g_hbm, sem.at[8])
    out_g.start()
    out_mid.wait()
    out_g.wait()


def spatial(cot, wos, wqkv_t, wot, q_t, k_t, v_t):
    heads, dim, tokens = q_t.shape
    features = cot.shape[1]
    channels = heads * dim
    any_spec = pl.BlockSpec(memory_space=pl.ANY)
    hbm_spec = pl.BlockSpec(memory_space=pltpu.HBM)
    ins = [cot, wos, wqkv_t, wot, q_t, k_t, v_t]
    return pl.pallas_call(
        spatial_kernel,
        out_shape=(
            jax.ShapeDtypeStruct((tokens, features), BF16),
            jax.ShapeDtypeStruct((tokens, channels), BF16),
        ),
        in_specs=[hbm_spec] * 7,
        out_specs=(hbm_spec, any_spec),
        scratch_shapes=[pltpu.VMEM(a.shape, BF16) for a in ins]
        + [
            pltpu.VMEM((heads, dim, tokens), F32),
            pltpu.VMEM((3 * heads, dim, tokens), BF16),
            pltpu.VMEM((tokens, features), BF16),
            pltpu.VMEM((tokens, channels), BF16),
            pltpu.SemaphoreType.DMA((9,)),
        ],
        compiler_params=pltpu.CompilerParams(vmem_limit_bytes=66 * 1000 * 1000),
        name="spatial",
    )(*ins)


def temporal_kernel(q_ref, k_ref, v_ref, g_ref, o_ref):
    frames, positions, channels = q_ref.shape
    dim = channels // HEADS
    scaling = dim ** (-0.5)
    exp_scale = scaling * LOG2E
    step = math.gcd(positions, 8)
    rows = frames * step
    row = lax.broadcasted_iota(jnp.int32, (rows, rows), 0)
    col = lax.broadcasted_iota(jnp.int32, (rows, rows), 1)
    bias = jnp.where(lax.rem(row, step) == lax.rem(col, step), 0.0, -1e30).astype(F32)
    for j in range(positions // step):
        at = pl.ds(j * step, step)

        def load(ref):
            return ref[:, at, :].astype(F32).reshape(rows, channels).astype(BF16)

        q, k, v, g = load(q_ref), load(k_ref), load(v_ref), load(g_ref)
        parts = [[], [], []]
        for h in range(HEADS):
            cut = slice(h * dim, (h + 1) * dim)
            q_h, k_h, v_h, g_h = q[:, cut], k[:, cut], v[:, cut], g[:, cut]
            scores = mm(k_h, q_h, NT) + bias
            top = jnp.max(scores, axis=0, keepdims=True)
            e = jnp.exp2((scores - top) * exp_scale)
            p = e * (1.0 / jnp.sum(e, axis=0, keepdims=True))
            grad_w = mm(v_h, g_h, NT)
            inner = jnp.sum(p * grad_w, axis=0, keepdims=True)
            ds = (p * (grad_w - inner)).astype(BF16)
            parts[0].append(mm(ds, k_h, TN) * scaling)
            parts[1].append(mm(ds, q_h, NN) * scaling)
            parts[2].append(mm(p.astype(BF16), g_h, NN))
        whole = jnp.concatenate(parts[0] + parts[1] + parts[2], axis=1)
        o_ref[:, at, :] = whole.reshape(frames, step, 3 * channels).astype(BF16)


def temporal(q, k, v, g):
    frames, positions, channels = q.shape
    return pl.pallas_call(
        temporal_kernel,
        out_shape=jax.ShapeDtypeStruct((frames, positions, 3 * channels), BF16),
        compiler_params=pltpu.CompilerParams(vmem_limit_bytes=32 << 20),
        name="temporal",
    )(q, k, v, g)


def local(cot, wos, wqkv, wot, qs, ks, vs, qt, kt, vt):
    tokens, features = cot.shape[1:]
    channels = qs.shape[2]
    dim = channels // HEADS
    axes = ("outer", "inner")
    groups = lax.axis_size(axes)
    pos_dev = tokens // groups

    def by_head(a):
        return a[0].T.reshape(HEADS, dim, tokens)

    middle, projected = spatial(
        cot[0], wos, wqkv.T, wot, by_head(qs), by_head(ks), by_head(vs)
    )
    temporal_out = lax.all_to_all(
        projected.reshape(groups, pos_dev, channels), axes, split_axis=0, concat_axis=0, tiled=True
    )
    stacked = temporal(qt, kt, vt, temporal_out)
    returned = lax.all_to_all(stacked, axes, split_axis=0, concat_axis=0, tiled=True)
    return (middle[None], returned.reshape(1, tokens, 3 * channels))


def solution(mesh):
    frame = P(("sample", "outer", "inner"), None, None)
    place = P("sample", ("outer", "inner"), None)
    return jax.shard_map(
        local,
        mesh=mesh,
        in_specs=(frame, P(), P(), P(), frame, frame, frame, place, place, place),
        out_specs=(frame, frame),
        check_vma=False,
    )
```

time: 97.4 us -> 82.5 us (0.85)
  matrix products: 23.6 us -> 0 us
  blocking collectives: 36.6 us -> 59.3 us
  Pallas kernels: 0 us -> 19.6 us
  local copies, waits for them, and re-layouts: 19.8 us -> 2.56 us
  starting transfers between devices: 8.35 us -> 0 us
  waiting for transfers between devices: 6.51 us -> 0 us
  other arithmetic: 1.24 us -> 0 us
    all_to_all x1 -> x2, blocking collectives: 36.6 us -> 59.3 us  [the longest x1 36.5 us: local(): lax.all_to_all(stacked, axes, split_axis=0, concat_axis=0, tiled=True)]
    pallas_call x0 -> x2, Pallas kernels: none -> 19.6 us  [the longest x1 13.2 us: spatial(): pl.pallas_call(spatial_kernel, out_shape=(jax.ShapeDtypeStruct((tokens, f...]
    dot_general x11 -> x0, matrix products: 16 us -> none  [the longest x2 6.55 us: attend_back(): jnp.einsum('lbhe,mbhe->bhlm', grad_out, value_rows, preferred_element_typ...]
    reshape x7 -> x0, local copies, waits for them, and re-layouts: 10.4 us -> none  [the longest x4 7.02 us: heads_view(): return array.reshape(length, batch, HEADS, array.shape[-1] // HEADS)]
    all_to_all x1 -> x0, starting transfers between devices: 8.35 us -> none  [local(): lax.all_to_all(projected.reshape(groups, pos_dev, channels), ('outer', 'i...]
    sub x2 -> x0, matrix products: 7.6 us -> none  [attend_back(): weights = jnp.exp(scores - row_max)]
    all_to_all x1 -> x0, waiting for transfers between devices: 6.51 us -> none  [local(): lax.all_to_all(projected.reshape(groups, pos_dev, channels), ('outer', 'i...]
    unnamed x29 -> x7, local copies, waits for them, and re-layouts: 5.52 us -> 2.56 us
  transfers between devices with their start and end apart: 1 -> 0, of which waited for: 1 -> 0; matrix products, arithmetic and copies ran while one was open for 8% -> 0% of each run, Pallas kernels for 0% -> 0%
where the time goes in v1:
time: 82.5 us; the launch traced here: 82.2 us
  blocking collectives  59.3 us (72%)
  Pallas kernels  19.6 us (24%)
  local copies, waits for them, and re-layouts  2.56 us (3%)
    all_to_all x1, blocking collectives, local(): lax.all_to_all(stacked, axes, split_axis=0, concat_axis=0, tiled=True)  36.5 us
    all_to_all x1, blocking collectives, local(): lax.all_to_all(projected.reshape(groups, pos_dev, channels), axes, split_...  22.9 us
    pallas_call x1, Pallas kernels, spatial(): pl.pallas_call(spatial_kernel, out_shape=(jax.ShapeDtypeStruct((tokens, f...  13.2 us
    pallas_call x1, Pallas kernels, temporal(): pl.pallas_call(temporal_kernel, out_shape=jax.ShapeDtypeStruct((frames, p...  6.44 us
    unnamed x7, local copies, waits for them, and re-layouts  2.56 us

profile of v1, /device:TPU:0, one launch (start us, length us, event | category | flops | bytes accessed | tf_op | source)
XLA Modules:
  0.0 82.2 jit_solution(5671784297146610211)
XLA Ops:
  0.6 0.0 copy-start
  0.6 0.0 copy-start.1
  0.7 13.2 %spatial.1 = (bf16[384,1152]{1,0:T(8,128)(2,1)}, bf16[384,576]{1,0:T(8,128)(2,1)}) custom-call(bf16[384,1152]{1,0:T(8,128)(2,1)} %bitcast.22, bf16[576,1152]{1,0:T(8,128)(2,1)} %wos_hbm.1, bf16[1728,1152]{1,0:T(8,128)(2,1)} %bitcast.21, bf16[576,1152]{1,0:T(8,128)(2,1)} %wot_hbm.1, bf16[8,72,384]{2,1,0:T(8,128)(2,1)} %bitcast.24, ...), custom_call_target="tpu_custom_call" | custom-call | tf_op jit(solution)/shard_map/spatial/pallas_call | solution.py:85
  13.8 22.9 %all_to_all.10.g_ref = bf16[16,24,576]{2,1,0:T(8,128)(2,1)S(1)} all-to-all(bf16[16,24,576]{2,1,0:T(8,128)(2,1)} %bitcast.23), channel_id=1, replica_groups=mesh['sample'=2,'outer'=2,'inner'=8] {'outer','inner'}, dimensions={0} | all-to-all | bytes 884736 | tf_op jit(solution)/shard_map/all_to_all | solution.py:165
  36.7 0.0 copy-done
  36.7 0.0 copy-done.1
  36.7 0.0 copy-start.2
  36.7 1.0 %copy-done.2 = bf16[16,24,576]{2,1,0:T(8,128)(2,1)S(1)} copy-done((bf16[16,24,576]{2,1,0:T(8,128)(2,1)S(1)}, bf16[16,24,576]{2,1,0:T(8,128)(2,1)}, u32[]{:S(2)}) %copy-start.2) | copy-done | bytes 442392
  37.7 6.4 %temporal.1 = bf16[16,24,1728]{2,1,0:T(8,128)(2,1)S(1)} custom-call(bf16[16,24,576]{2,1,0:T(8,128)(2,1)S(1)} %copy-done, bf16[16,24,576]{2,1,0:T(8,128)(2,1)S(1)} %copy-done.1, bf16[16,24,576]{2,1,0:T(8,128)(2,1)S(1)} %copy-done.2, bf16[16,24,576]{2,1,0:T(8,128)(2,1)S(1)} %all_to_all.10.g_ref), custom_call_target="tpu_custom_call" | custom-call | tf_op jit(solution)/shard_map/temporal/pallas_call | solution.py:143
  44.2 36.5 %all_to_all.11 = bf16[16,24,1728]{2,1,0:T(8,128)(2,1)S(1)} all-to-all(bf16[16,24,1728]{2,1,0:T(8,128)(2,1)S(1)} %temporal.1), channel_id=1, replica_groups=mesh['sample'=2,'outer'=2,'inner'=8] {'outer','inner'}, dimensions={0} | all-to-all | bytes 2654208 | tf_op jit(solution)/shard_map/all_to_all | solution.py:169
  80.6 1.5 %copy.12 = bf16[1,384,1728]{1,2,0:T(8,128)(2,1)} copy(bf16[1,384,1728]{2,1,0:T(8,128)(2,1)S(1)} %bitcast.20) | data formatting | bytes 2654208
Async XLA Ops:
  0.6 36.1 %copy-start = (bf16[16,24,576]{2,1,0:T(8,128)(2,1)S(1)}, bf16[16,24,576]{2,1,0:T(8,128)(2,1)}, u32[]{:S(2)}) copy-start(bf16[16,24,576]{2,1,0:T(8,128)(2,1)} %q_ref.1) | copy-start | bytes 1327108
  0.6 36.1 %copy-start.1 = (bf16[16,24,576]{2,1,0:T(8,128)(2,1)S(1)}, bf16[16,24,576]{2,1,0:T(8,128)(2,1)}, u32[]{:S(2)}) copy-start(bf16[16,24,576]{2,1,0:T(8,128)(2,1)} %k_ref.1) | copy-start | bytes 1327108
  36.7 1.0 %copy-start.2 = (bf16[16,24,576]{2,1,0:T(8,128)(2,1)S(1)}, bf16[16,24,576]{2,1,0:T(8,128)(2,1)}, u32[]{:S(2)}) copy-start(bf16[16,24,576]{2,1,0:T(8,128)(2,1)} %v_ref.1) | copy-start | bytes 1327108
